TPU v7x, 256 devices: a whole 4x4x8 slice. The times are simulated.
256 devices in a mesh: seq: 32 (over z, y), exp: 4 (over x), dp: 2 (over core).
Axes of the slice: x: 4, y: 4, z: 8, core: 2. Of those that a mesh axis runs over, the one named last changes fastest.
Arguments:
- head_inputs: bfloat16 [16384, 4096], P(('dp', 'seq'), 'exp'), parts along dimension 0, may hold values from -6 to 6
- input_matrix: bfloat16 [16384, 128], P(('dp', 'seq')), parts along dimension 0, may hold values from -0.015625 to 0.015625
- output_matrix: bfloat16 [16384, 128], P(('dp', 'seq')), parts along dimension 0, may hold values from -6 to 6
- log_decay: float32 [64, 16384], P('exp', ('dp', 'seq')), parts along dimension 1, may hold values from -1 to 0
- skip_gain: float32 [64], P('exp'), may hold values from 0.5 to 1.5
- residual: bfloat16 [16384, 4096], P(('dp', 'seq', 'exp')), parts along dimension 0, may hold values from -6 to 6
- norm_gain: float32 [4096], replicated, may hold values from 0.1 to 1.9
- router_weight: bfloat16 [4096, 16], replicated, may hold values from -0.09375 to 0.09375
- expert_ids: int32 [16384, 2], P(('dp', 'seq', 'exp')), parts along dimension 0, may hold values from 0 to 15, as said below
- gate_weight: bfloat16 [4, 4096, 12288], P('exp', None, 'seq'), may hold values from -0.09375 to 0.09375
- up_weight: bfloat16 [4, 4096, 12288], P('exp', None, 'seq'), may hold values from -0.09375 to 0.09375
- down_weight: bfloat16 [4, 12288, 4096], P('exp', 'seq'), may hold values from -0.0546875 to 0.0546875
Outputs:
- layer_out: bfloat16 [16384, 4096], P(('dp', 'seq', 'exp')), parts along dimension 0
There are 2 independent parts, one for each index of `dp`. A program takes and returns all parts, laid end to end along the dimension named above; an argument that names none is the same for every part. Nothing has to cross between parts.
Inputs may be any that keep to these rules, and one draw needn't show every extreme that they name: `expert_ids`: each row names two different experts; the second column never names an expert below 4. In every aligned block of 64 rows each expert below 4 is named by at most 8 rows, and in every run of 4 consecutive blocks, starting at block 0, by at most 16 rows; in every run one such expert is named by exactly 8 rows in one block and by exactly 16 rows in the whole run.
All inputs are finite; a program needn't handle non-finite values.
Results may differ from a plain program's by a relative error of at most 0.015.
Values may be sent and summed in bfloat16 or wider, within the bound.
A program may use at most 128 MiB of HBM per device.

v0:
```python
import jax
import jax.numpy as jnp
from jax import lax
from jax.sharding import PartitionSpec as P

P_SIZE = 64
CAP = 8


def shifted(block, axis, distance):
    devices = range(lax.axis_size(axis))
    route = [(i - distance, i) for i in devices if i - distance in devices]
    return lax.ppermute(block, axis, route)


def body(
    head_inputs,
    input_matrix,
    output_matrix,
    log_decay,
    skip_gain,
    residual,
    norm_gain,
    router_weight,
    expert_ids,
    gate_weight,
    up_weight,
    down_weight,
):
    length = head_inputs.shape[0]
    heads = log_decay.shape[0]
    per_head = head_inputs.reshape(length, heads, P_SIZE)
    cumulative = jnp.cumsum(log_decay, axis=1)
    scores = jnp.dot(output_matrix, input_matrix.T, preferred_element_type=jnp.float32)
    causal = lax.broadcasted_iota(jnp.int32, (length, length), 0) >= lax.broadcasted_iota(
        jnp.int32, (length, length), 1
    )
    spread = jnp.minimum(cumulative[:, :, None] - cumulative[:, None, :], 0.0)
    mixing = jnp.where(causal[None], jnp.exp(spread) * scores[None], 0.0).astype(jnp.bfloat16)
    within = jnp.einsum("hts,shp->thp", mixing, per_head, preferred_element_type=jnp.float32)
    remain = jnp.exp(cumulative[:, -1:] - cumulative)
    weighted = (remain[:, :, None] * input_matrix.astype(jnp.float32)[None]).astype(jnp.bfloat16)
    local_state = jnp.einsum("shp,hsn->hpn", per_head, weighted, preferred_element_type=jnp.float32)
    block_decay = jnp.exp(cumulative[:, -1])

    def advance(iteration, incoming):
        outgoing = block_decay[:, None, None] * incoming + local_state
        return shifted(outgoing.astype(jnp.bfloat16), "seq", 1).astype(outgoing.dtype)

    entering = lax.fori_loop(0, lax.axis_size("seq") - 1, advance, jnp.zeros_like(local_state))
    carried = jnp.einsum(
        "tn,hpn->thp", output_matrix.astype(jnp.float32), entering, precision=lax.Precision.HIGHEST
    )
    carried = carried * jnp.exp(cumulative).T[:, :, None]
    mixed = within + carried + skip_gain[None, :, None] * per_head.astype(jnp.float32)
    mamba_out = mixed.reshape(length, heads * P_SIZE).astype(jnp.bfloat16)
    token_rows = lax.all_to_all(mamba_out, "exp", split_axis=0, concat_axis=1, tiled=True)
    stream = (residual.astype(jnp.float32) + token_rows.astype(jnp.float32)).astype(jnp.bfloat16)
    stream_wide = stream.astype(jnp.float32)
    normed = (
        stream_wide
        * lax.rsqrt(jnp.mean(stream_wide * stream_wide, axis=-1, keepdims=True) + 1e-06)
        * norm_gain
    ).astype(jnp.bfloat16)
    logits = jnp.dot(normed, router_weight, preferred_element_type=jnp.float32)
    expert_iota = lax.broadcasted_iota(jnp.int32, logits.shape, 1)
    first = expert_ids[:, 0]
    second = expert_ids[:, 1]
    first_logit = jnp.sum(jnp.where(expert_iota == first[:, None], logits, 0.0), axis=-1)
    second_logit = jnp.sum(jnp.where(expert_iota == second[:, None], logits, 0.0), axis=-1)
    gate = jax.nn.sigmoid(first_logit - second_logit)
    flight = lax.axis_size("exp")
    member = (first[:, None] == jnp.arange(flight, dtype=jnp.int32)[None, :]).astype(jnp.int32)
    ranking = jnp.cumsum(member, axis=0) - member
    slots = jnp.sum(ranking * member, axis=-1)
    chosen = (member.T[:, None, :] == 1) & (
        slots[None, None, :] == jnp.arange(CAP, dtype=jnp.int32)[None, :, None]
    )
    select = chosen.astype(jnp.bfloat16)
    outbound = jnp.einsum("ecr,rd->ecd", select, normed, preferred_element_type=jnp.float32).astype(
        jnp.bfloat16
    )
    model_width = outbound.shape[2]
    inbound = lax.all_to_all(outbound, "exp", split_axis=0, concat_axis=0, tiled=True)
    routed = inbound.reshape(flight * CAP, model_width)
    gate_part = gate_weight[0]
    up_part = up_weight[0]
    down_part = down_weight[0]
    fragment = lax.all_gather(routed, "seq", axis=0, tiled=True)
    gated = jnp.dot(fragment, gate_part, preferred_element_type=jnp.float32)
    lifted = jnp.dot(fragment, up_part, preferred_element_type=jnp.float32)
    hidden_all = (jax.nn.silu(gated) * lifted).astype(jnp.bfloat16)
    fragment = hidden_all
    summed = lax.psum_scatter(
        jnp.dot(fragment, down_part, preferred_element_type=jnp.float32).astype(jnp.bfloat16),
        "seq",
        scatter_dimension=0,
        tiled=True,
    )
    expert_out = summed.reshape(flight, CAP, model_width)
    returned = lax.all_to_all(expert_out, "exp", split_axis=0, concat_axis=0, tiled=True)
    combined = jnp.einsum("ecr,ecd->rd", select, returned, preferred_element_type=jnp.float32)
    return (stream_wide + gate[:, None] * combined).astype(jnp.bfloat16)


def solution(mesh):
    return jax.shard_map(
        body,
        mesh=mesh,
        in_specs=(
            P(("dp", "seq"), "exp"),
            P(("dp", "seq"), None),
            P(("dp", "seq"), None),
            P("exp", ("dp", "seq")),
            P("exp"),
            P(("dp", "seq", "exp"), None),
            P(),
            P(),
            P(("dp", "seq", "exp"), None),
            P("exp", None, "seq"),
            P("exp", None, "seq"),
            P("exp", "seq", None),
        ),
        out_specs=P(("dp", "seq", "exp"), None),
        check_vma=False,
    )
```

profile of v0, /device:TPU:64, one launch (start us, length us, event | category | flops | bytes accessed | tf_op | source)
XLA Modules:
  0.0 889.1 jit_solution(8230713345053279905)
XLA Ops:
  14.3 2.7 convolution_bitcast_fusion.2
  16.9 3.3 fusion.18
  20.3 442.0 %while.11 = (s32[]{:T(128)}, f32[16,64,128]{2,1,0:T(8,128)}, f32[16]{0:T(128)S(1)}, f32[16,64,128]{2,1,0:T(8,128)}, s32[]{:T(128)}, /*index=5*/s32[]{:T(128)}) while((s32[]{:T(128)}, f32[16,64,128]{2,1,0:T(8,128)}, f32[16]{0:T(128)S(1)}, f32[16,64,128]{2,1,0:T(8,128)}, s32[]{:T(128)}, /*index=5*/s32[]{:T(128)}) %tuple.33), condition=%wide.region_3.4_spmd.clone, body=%wide.region_2.3_spmd.clone.sunk | while | flops 655363 | bytes 3145911 | solution.py:50
  22.2 3.5 collective-permute-start
  25.7 8.8 collective-permute-done
  35.3 2.1 fusion.54
  39.3 9.5 %collective-permute-done = bf16[16,64,128]{2,1,0:T(8,128)(2,1)S(1)} collective-permute-done((bf16[16,64,128]{2,1,0:T(8,128)(2,1)}, bf16[16,64,128]{2,1,0:T(8,128)(2,1)S(1)}, u32[]{:S(2)}, u32[]{:S(2)}) %collective-permute-start) | collective-permute-done | bytes 262176 | tf_op jit(solution)/shard_map/while/body/eval_jaxpr/ppermute | solution.py:13
  53.6 8.7 collective-permute-done
  67.1 8.7 collective-permute-done
  76.6 2.1 fusion.54
  80.6 8.7 collective-permute-done
  90.1 2.1 fusion.54
  94.0 8.7 collective-permute-done
  103.6 2.1 fusion.54
  107.5 8.7 collective-permute-done
  117.1 2.1 fusion.54
  121.0 8.7 collective-permute-done
  130.5 2.1 fusion.54
  134.5 8.9 collective-permute-done
  144.2 2.1 fusion.54
  148.2 10.0 %collective-permute-done = bf16[16,64,128]{2,1,0:T(8,128)(2,1)S(1)} collective-permute-done((bf16[16,64,128]{2,1,0:T(8,128)(2,1)}, bf16[16,64,128]{2,1,0:T(8,128)(2,1)S(1)}, u32[]{:S(2)}, u32[]{:S(2)}) %collective-permute-start) | collective-permute-done | bytes 262176 | tf_op jit(solution)/shard_map/while/body/eval_jaxpr/ppermute | solution.py:13
  159.1 2.1 fusion.54
  163.1 11.2 %collective-permute-done = bf16[16,64,128]{2,1,0:T(8,128)(2,1)S(1)} collective-permute-done((bf16[16,64,128]{2,1,0:T(8,128)(2,1)}, bf16[16,64,128]{2,1,0:T(8,128)(2,1)S(1)}, u32[]{:S(2)}, u32[]{:S(2)}) %collective-permute-start) | collective-permute-done | bytes 262176 | tf_op jit(solution)/shard_map/while/body/eval_jaxpr/ppermute | solution.py:13
  175.1 2.1 fusion.54
  179.0 10.6 %collective-permute-done = bf16[16,64,128]{2,1,0:T(8,128)(2,1)S(1)} collective-permute-done((bf16[16,64,128]{2,1,0:T(8,128)(2,1)}, bf16[16,64,128]{2,1,0:T(8,128)(2,1)S(1)}, u32[]{:S(2)}, u32[]{:S(2)}) %collective-permute-start) | collective-permute-done | bytes 262176 | tf_op jit(solution)/shard_map/while/body/eval_jaxpr/ppermute | solution.py:13
  190.5 2.1 fusion.54
  194.5 9.8 %collective-permute-done = bf16[16,64,128]{2,1,0:T(8,128)(2,1)S(1)} collective-permute-done((bf16[16,64,128]{2,1,0:T(8,128)(2,1)}, bf16[16,64,128]{2,1,0:T(8,128)(2,1)S(1)}, u32[]{:S(2)}, u32[]{:S(2)}) %collective-permute-start) | collective-permute-done | bytes 262176 | tf_op jit(solution)/shard_map/while/body/eval_jaxpr/ppermute | solution.py:13
  209.1 8.9 %collective-permute-done = bf16[16,64,128]{2,1,0:T(8,128)(2,1)S(1)} collective-permute-done((bf16[16,64,128]{2,1,0:T(8,128)(2,1)}, bf16[16,64,128]{2,1,0:T(8,128)(2,1)S(1)}, u32[]{:S(2)}, u32[]{:S(2)}) %collective-permute-start) | collective-permute-done | bytes 262176 | tf_op jit(solution)/shard_map/while/body/eval_jaxpr/ppermute | solution.py:13
  222.8 8.7 collective-permute-done
  236.3 8.7 collective-permute-done
  249.8 8.7 collective-permute-done
  263.3 8.7 collective-permute-done
  276.8 8.7 collective-permute-done
  290.3 8.7 collective-permute-done
  303.8 9.4 %collective-permute-done = bf16[16,64,128]{2,1,0:T(8,128)(2,1)S(1)} collective-permute-done((bf16[16,64,128]{2,1,0:T(8,128)(2,1)}, bf16[16,64,128]{2,1,0:T(8,128)(2,1)S(1)}, u32[]{:S(2)}, u32[]{:S(2)}) %collective-permute-start) | collective-permute-done | bytes 262176 | tf_op jit(solution)/shard_map/while/body/eval_jaxpr/ppermute | solution.py:13
  318.0 10.6 %collective-permute-done = bf16[16,64,128]{2,1,0:T(8,128)(2,1)S(1)} collective-permute-done((bf16[16,64,128]{2,1,0:T(8,128)(2,1)}, bf16[16,64,128]{2,1,0:T(8,128)(2,1)S(1)}, u32[]{:S(2)}, u32[]{:S(2)}) %collective-permute-start) | collective-permute-done | bytes 262176 | tf_op jit(solution)/shard_map/while/body/eval_jaxpr/ppermute | solution.py:13
  333.4 11.2 %collective-permute-done = bf16[16,64,128]{2,1,0:T(8,128)(2,1)S(1)} collective-permute-done((bf16[16,64,128]{2,1,0:T(8,128)(2,1)}, bf16[16,64,128]{2,1,0:T(8,128)(2,1)S(1)}, u32[]{:S(2)}, u32[]{:S(2)}) %collective-permute-start) | collective-permute-done | bytes 262176 | tf_op jit(solution)/shard_map/while/body/eval_jaxpr/ppermute | solution.py:13
  349.5 10.3 %collective-permute-done = bf16[16,64,128]{2,1,0:T(8,128)(2,1)S(1)} collective-permute-done((bf16[16,64,128]{2,1,0:T(8,128)(2,1)}, bf16[16,64,128]{2,1,0:T(8,128)(2,1)S(1)}, u32[]{:S(2)}, u32[]{:S(2)}) %collective-permute-start) | collective-permute-done | bytes 262176 | tf_op jit(solution)/shard_map/while/body/eval_jaxpr/ppermute | solution.py:13
  364.7 9.5 %collective-permute-done = bf16[16,64,128]{2,1,0:T(8,128)(2,1)S(1)} collective-permute-done((bf16[16,64,128]{2,1,0:T(8,128)(2,1)}, bf16[16,64,128]{2,1,0:T(8,128)(2,1)S(1)}, u32[]{:S(2)}, u32[]{:S(2)}) %collective-permute-start) | collective-permute-done | bytes 262176 | tf_op jit(solution)/shard_map/while/body/eval_jaxpr/ppermute | solution.py:13
  379.0 8.7 collective-permute-done
  390.5 3.4 collective-permute-start
  393.9 7.2 collective-permute-done
  404.0 7.7 collective-permute-start
  411.7 5.5 collective-permute-done
  420.1 8.0 collective-permute-start
  428.1 4.3 collective-permute-done
  435.3 7.5 collective-permute-start
  442.8 4.2 collective-permute-done
  449.9 7.3 collective-permute-start
  457.2 4.2 collective-permute-done
  462.2 2.9 fusion.22
  465.2 2.8 reshape.161
  467.9 2.3 copy.30
  470.2 4.3 all-to-all-start
  474.9 7.8 all-to-all-done
  485.4 9.7 %all_to_all.20 = bf16[4,8,4096]{2,1,0:T(8,128)(2,1)} all-to-all(bf16[4,8,4096]{2,1,0:T(8,128)(2,1)S(1)} %convolution_convert_fusion.1), channel_id=1, replica_groups=mesh['seq'=32,'exp'=4,'dp'=2] {'exp'}, dimensions={0} | all-to-all | bytes 524288 | tf_op jit(solution)/shard_map/all_to_all | solution.py:84
  495.2 126.1 %all-gather.2.cloned.1.call-done = bf16[1024,4096]{1,0:T(8,128)(2,1)} async-done(((bf16[32,4096]{1,0:T(8,128)(2,1)}), bf16[1024,4096]{1,0:T(8,128)(2,1)}) %all-gather.2.cloned.1.call-update) | async-done | bytes 8388624 | tf_op jit(solution)/shard_map/all_gather | solution.py:89
  621.3 8.0 fusion.8
  629.3 4.6 multiply_convert_fusion.1
  633.9 6.7 convolution_convert_fusion
  642.9 226.2 %reduce-scatter.2.cloned.1.call-done = bf16[32,4096]{1,0:T(8,128)(2,1)} async-done(((bf16[1024,4096]{1,0:T(8,128)(2,1)}), bf16[32,4096]{1,0:T(8,128)(2,1)}) %reduce-scatter.2.cloned.1.call-update) | async-done | bytes 262160 | tf_op jit(solution)/shard_map/reduce_scatter | solution.py:94
  869.1 4.3 all-to-all-start.2
  873.4 6.7 all-to-all-done.2
  880.0 2.2 fusion.4
  (132 shorter events, 130.4 us)
Async XLA Ops:
  6.5 627.4 %copy-start = (bf16[1,384,4096]{2,1,0:T(8,128)(2,1)S(1)}, bf16[1,384,4096]{2,1,0:T(8,128)(2,1)}, u32[]{:S(2)}) copy-start(bf16[1,384,4096]{2,1,0:T(8,128)(2,1)} %param.25) | copy-start | bytes 9437188
  8.3 1.4 copy-start.4
  16.9 3.3 copy-start.5
  20.2 442.0 %copy-start.3 = (bf16[256,128]{1,0:T(8,128)(2,1)S(1)}, bf16[256,128]{1,0:T(8,128)(2,1)}, u32[]{:S(2)}) copy-start(bf16[256,128]{1,0:T(8,128)(2,1)} %param.16) | copy-start | bytes 196612
  20.3 442.0 %copy-start.7 = (f32[16]{0:T(128)S(1)}, f32[16]{0:T(128)}, u32[]{:S(2)}) copy-start(f32[16]{0:T(128)} %param.18) | copy-start | bytes 196
  22.2 12.2 %collective-permute-start = (bf16[16,64,128]{2,1,0:T(8,128)(2,1)}, bf16[16,64,128]{2,1,0:T(8,128)(2,1)S(1)}, u32[]{:S(2)}, u32[]{:S(2)}) collective-permute-start(bf16[16,64,128]{2,1,0:T(8,128)(2,1)} %fusion.54), channel_id=1, source_target_pairs={{0,8},{8,16},{16,24},{24,32},{32,40},{40,48},{48,56},{56,64},{64,7... | collective-permute-start | bytes 786440 | tf_op jit(solution)/shard_map/while/body/eval_jaxpr/ppermute | solution.py:13
  37.4 11.4 %collective-permute-start = (bf16[16,64,128]{2,1,0:T(8,128)(2,1)}, bf16[16,64,128]{2,1,0:T(8,128)(2,1)S(1)}, u32[]{:S(2)}, u32[]{:S(2)}) collective-permute-start(bf16[16,64,128]{2,1,0:T(8,128)(2,1)} %fusion.54), channel_id=1, source_target_pairs={{0,8},{8,16},{16,24},{24,32},{32,40},{40,48},{48,56},{56,64},{64,7... | collective-permute-start | bytes 786440 | tf_op jit(solution)/shard_map/while/body/eval_jaxpr/ppermute | solution.py:13
  51.7 10.6 %collective-permute-start = (bf16[16,64,128]{2,1,0:T(8,128)(2,1)}, bf16[16,64,128]{2,1,0:T(8,128)(2,1)S(1)}, u32[]{:S(2)}, u32[]{:S(2)}) collective-permute-start(bf16[16,64,128]{2,1,0:T(8,128)(2,1)} %fusion.54), channel_id=1, source_target_pairs={{0,8},{8,16},{16,24},{24,32},{32,40},{40,48},{48,56},{56,64},{64,7... | collective-permute-start | bytes 786440 | tf_op jit(solution)/shard_map/while/body/eval_jaxpr/ppermute | solution.py:13
  65.2 10.6 %collective-permute-start = (bf16[16,64,128]{2,1,0:T(8,128)(2,1)}, bf16[16,64,128]{2,1,0:T(8,128)(2,1)S(1)}, u32[]{:S(2)}, u32[]{:S(2)}) collective-permute-start(bf16[16,64,128]{2,1,0:T(8,128)(2,1)} %fusion.54), channel_id=1, source_target_pairs={{0,8},{8,16},{16,24},{24,32},{32,40},{40,48},{48,56},{56,64},{64,7... | collective-permute-start | bytes 786440 | tf_op jit(solution)/shard_map/while/body/eval_jaxpr/ppermute | solution.py:13
  78.6 10.6 %collective-permute-start = (bf16[16,64,128]{2,1,0:T(8,128)(2,1)}, bf16[16,64,128]{2,1,0:T(8,128)(2,1)S(1)}, u32[]{:S(2)}, u32[]{:S(2)}) collective-permute-start(bf16[16,64,128]{2,1,0:T(8,128)(2,1)} %fusion.54), channel_id=1, source_target_pairs={{0,8},{8,16},{16,24},{24,32},{32,40},{40,48},{48,56},{56,64},{64,7... | collective-permute-start | bytes 786440 | tf_op jit(solution)/shard_map/while/body/eval_jaxpr/ppermute | solution.py:13
  92.1 10.6 %collective-permute-start = (bf16[16,64,128]{2,1,0:T(8,128)(2,1)}, bf16[16,64,128]{2,1,0:T(8,128)(2,1)S(1)}, u32[]{:S(2)}, u32[]{:S(2)}) collective-permute-start(bf16[16,64,128]{2,1,0:T(8,128)(2,1)} %fusion.54), channel_id=1, source_target_pairs={{0,8},{8,16},{16,24},{24,32},{32,40},{40,48},{48,56},{56,64},{64,7... | collective-permute-start | bytes 786440 | tf_op jit(solution)/shard_map/while/body/eval_jaxpr/ppermute | solution.py:13
  105.6 10.6 %collective-permute-start = (bf16[16,64,128]{2,1,0:T(8,128)(2,1)}, bf16[16,64,128]{2,1,0:T(8,128)(2,1)S(1)}, u32[]{:S(2)}, u32[]{:S(2)}) collective-permute-start(bf16[16,64,128]{2,1,0:T(8,128)(2,1)} %fusion.54), channel_id=1, source_target_pairs={{0,8},{8,16},{16,24},{24,32},{32,40},{40,48},{48,56},{56,64},{64,7... | collective-permute-start | bytes 786440 | tf_op jit(solution)/shard_map/while/body/eval_jaxpr/ppermute | solution.py:13
  119.1 10.6 %collective-permute-start = (bf16[16,64,128]{2,1,0:T(8,128)(2,1)}, bf16[16,64,128]{2,1,0:T(8,128)(2,1)S(1)}, u32[]{:S(2)}, u32[]{:S(2)}) collective-permute-start(bf16[16,64,128]{2,1,0:T(8,128)(2,1)} %fusion.54), channel_id=1, source_target_pairs={{0,8},{8,16},{16,24},{24,32},{32,40},{40,48},{48,56},{56,64},{64,7... | collective-permute-start | bytes 786440 | tf_op jit(solution)/shard_map/while/body/eval_jaxpr/ppermute | solution.py:13
  132.6 10.8 %collective-permute-start = (bf16[16,64,128]{2,1,0:T(8,128)(2,1)}, bf16[16,64,128]{2,1,0:T(8,128)(2,1)S(1)}, u32[]{:S(2)}, u32[]{:S(2)}) collective-permute-start(bf16[16,64,128]{2,1,0:T(8,128)(2,1)} %fusion.54), channel_id=1, source_target_pairs={{0,8},{8,16},{16,24},{24,32},{32,40},{40,48},{48,56},{56,64},{64,7... | collective-permute-start | bytes 786440 | tf_op jit(solution)/shard_map/while/body/eval_jaxpr/ppermute | solution.py:13
  146.3 11.9 %collective-permute-start = (bf16[16,64,128]{2,1,0:T(8,128)(2,1)}, bf16[16,64,128]{2,1,0:T(8,128)(2,1)S(1)}, u32[]{:S(2)}, u32[]{:S(2)}) collective-permute-start(bf16[16,64,128]{2,1,0:T(8,128)(2,1)} %fusion.54), channel_id=1, source_target_pairs={{0,8},{8,16},{16,24},{24,32},{32,40},{40,48},{48,56},{56,64},{64,7... | collective-permute-start | bytes 786440 | tf_op jit(solution)/shard_map/while/body/eval_jaxpr/ppermute | solution.py:13
  161.1 13.1 %collective-permute-start = (bf16[16,64,128]{2,1,0:T(8,128)(2,1)}, bf16[16,64,128]{2,1,0:T(8,128)(2,1)S(1)}, u32[]{:S(2)}, u32[]{:S(2)}) collective-permute-start(bf16[16,64,128]{2,1,0:T(8,128)(2,1)} %fusion.54), channel_id=1, source_target_pairs={{0,8},{8,16},{16,24},{24,32},{32,40},{40,48},{48,56},{56,64},{64,7... | collective-permute-start | bytes 786440 | tf_op jit(solution)/shard_map/while/body/eval_jaxpr/ppermute | solution.py:13
  177.1 12.5 %collective-permute-start = (bf16[16,64,128]{2,1,0:T(8,128)(2,1)}, bf16[16,64,128]{2,1,0:T(8,128)(2,1)S(1)}, u32[]{:S(2)}, u32[]{:S(2)}) collective-permute-start(bf16[16,64,128]{2,1,0:T(8,128)(2,1)} %fusion.54), channel_id=1, source_target_pairs={{0,8},{8,16},{16,24},{24,32},{32,40},{40,48},{48,56},{56,64},{64,7... | collective-permute-start | bytes 786440 | tf_op jit(solution)/shard_map/while/body/eval_jaxpr/ppermute | solution.py:13
  192.6 11.7 %collective-permute-start = (bf16[16,64,128]{2,1,0:T(8,128)(2,1)}, bf16[16,64,128]{2,1,0:T(8,128)(2,1)S(1)}, u32[]{:S(2)}, u32[]{:S(2)}) collective-permute-start(bf16[16,64,128]{2,1,0:T(8,128)(2,1)} %fusion.54), channel_id=1, source_target_pairs={{0,8},{8,16},{16,24},{24,32},{32,40},{40,48},{48,56},{56,64},{64,7... | collective-permute-start | bytes 786440 | tf_op jit(solution)/shard_map/while/body/eval_jaxpr/ppermute | solution.py:13
  207.2 10.8 %collective-permute-start = (bf16[16,64,128]{2,1,0:T(8,128)(2,1)}, bf16[16,64,128]{2,1,0:T(8,128)(2,1)S(1)}, u32[]{:S(2)}, u32[]{:S(2)}) collective-permute-start(bf16[16,64,128]{2,1,0:T(8,128)(2,1)} %fusion.54), channel_id=1, source_target_pairs={{0,8},{8,16},{16,24},{24,32},{32,40},{40,48},{48,56},{56,64},{64,7... | collective-permute-start | bytes 786440 | tf_op jit(solution)/shard_map/while/body/eval_jaxpr/ppermute | solution.py:13
  220.9 10.6 %collective-permute-start = (bf16[16,64,128]{2,1,0:T(8,128)(2,1)}, bf16[16,64,128]{2,1,0:T(8,128)(2,1)S(1)}, u32[]{:S(2)}, u32[]{:S(2)}) collective-permute-start(bf16[16,64,128]{2,1,0:T(8,128)(2,1)} %fusion.54), channel_id=1, source_target_pairs={{0,8},{8,16},{16,24},{24,32},{32,40},{40,48},{48,56},{56,64},{64,7... | collective-permute-start | bytes 786440 | tf_op jit(solution)/shard_map/while/body/eval_jaxpr/ppermute | solution.py:13
  234.4 10.6 %collective-permute-start = (bf16[16,64,128]{2,1,0:T(8,128)(2,1)}, bf16[16,64,128]{2,1,0:T(8,128)(2,1)S(1)}, u32[]{:S(2)}, u32[]{:S(2)}) collective-permute-start(bf16[16,64,128]{2,1,0:T(8,128)(2,1)} %fusion.54), channel_id=1, source_target_pairs={{0,8},{8,16},{16,24},{24,32},{32,40},{40,48},{48,56},{56,64},{64,7... | collective-permute-start | bytes 786440 | tf_op jit(solution)/shard_map/while/body/eval_jaxpr/ppermute | solution.py:13
  247.9 10.6 %collective-permute-start = (bf16[16,64,128]{2,1,0:T(8,128)(2,1)}, bf16[16,64,128]{2,1,0:T(8,128)(2,1)S(1)}, u32[]{:S(2)}, u32[]{:S(2)}) collective-permute-start(bf16[16,64,128]{2,1,0:T(8,128)(2,1)} %fusion.54), channel_id=1, source_target_pairs={{0,8},{8,16},{16,24},{24,32},{32,40},{40,48},{48,56},{56,64},{64,7... | collective-permute-start | bytes 786440 | tf_op jit(solution)/shard_map/while/body/eval_jaxpr/ppermute | solution.py:13
  261.4 10.6 %collective-permute-start = (bf16[16,64,128]{2,1,0:T(8,128)(2,1)}, bf16[16,64,128]{2,1,0:T(8,128)(2,1)S(1)}, u32[]{:S(2)}, u32[]{:S(2)}) collective-permute-start(bf16[16,64,128]{2,1,0:T(8,128)(2,1)} %fusion.54), channel_id=1, source_target_pairs={{0,8},{8,16},{16,24},{24,32},{32,40},{40,48},{48,56},{56,64},{64,7... | collective-permute-start | bytes 786440 | tf_op jit(solution)/shard_map/while/body/eval_jaxpr/ppermute | solution.py:13
  274.9 10.6 %collective-permute-start = (bf16[16,64,128]{2,1,0:T(8,128)(2,1)}, bf16[16,64,128]{2,1,0:T(8,128)(2,1)S(1)}, u32[]{:S(2)}, u32[]{:S(2)}) collective-permute-start(bf16[16,64,128]{2,1,0:T(8,128)(2,1)} %fusion.54), channel_id=1, source_target_pairs={{0,8},{8,16},{16,24},{24,32},{32,40},{40,48},{48,56},{56,64},{64,7... | collective-permute-start | bytes 786440 | tf_op jit(solution)/shard_map/while/body/eval_jaxpr/ppermute | solution.py:13
  288.4 10.6 %collective-permute-start = (bf16[16,64,128]{2,1,0:T(8,128)(2,1)}, bf16[16,64,128]{2,1,0:T(8,128)(2,1)S(1)}, u32[]{:S(2)}, u32[]{:S(2)}) collective-permute-start(bf16[16,64,128]{2,1,0:T(8,128)(2,1)} %fusion.54), channel_id=1, source_target_pairs={{0,8},{8,16},{16,24},{24,32},{32,40},{40,48},{48,56},{56,64},{64,7... | collective-permute-start | bytes 786440 | tf_op jit(solution)/shard_map/while/body/eval_jaxpr/ppermute | solution.py:13
  301.9 11.3 %collective-permute-start = (bf16[16,64,128]{2,1,0:T(8,128)(2,1)}, bf16[16,64,128]{2,1,0:T(8,128)(2,1)S(1)}, u32[]{:S(2)}, u32[]{:S(2)}) collective-permute-start(bf16[16,64,128]{2,1,0:T(8,128)(2,1)} %fusion.54), channel_id=1, source_target_pairs={{0,8},{8,16},{16,24},{24,32},{32,40},{40,48},{48,56},{56,64},{64,7... | collective-permute-start | bytes 786440 | tf_op jit(solution)/shard_map/while/body/eval_jaxpr/ppermute | solution.py:13
  316.1 12.5 %collective-permute-start = (bf16[16,64,128]{2,1,0:T(8,128)(2,1)}, bf16[16,64,128]{2,1,0:T(8,128)(2,1)S(1)}, u32[]{:S(2)}, u32[]{:S(2)}) collective-permute-start(bf16[16,64,128]{2,1,0:T(8,128)(2,1)} %fusion.54), channel_id=1, source_target_pairs={{0,8},{8,16},{16,24},{24,32},{32,40},{40,48},{48,56},{56,64},{64,7... | collective-permute-start | bytes 786440 | tf_op jit(solution)/shard_map/while/body/eval_jaxpr/ppermute | solution.py:13
  331.5 13.1 %collective-permute-start = (bf16[16,64,128]{2,1,0:T(8,128)(2,1)}, bf16[16,64,128]{2,1,0:T(8,128)(2,1)S(1)}, u32[]{:S(2)}, u32[]{:S(2)}) collective-permute-start(bf16[16,64,128]{2,1,0:T(8,128)(2,1)} %fusion.54), channel_id=1, source_target_pairs={{0,8},{8,16},{16,24},{24,32},{32,40},{40,48},{48,56},{56,64},{64,7... | collective-permute-start | bytes 786440 | tf_op jit(solution)/shard_map/while/body/eval_jaxpr/ppermute | solution.py:13
  347.6 12.3 %collective-permute-start = (bf16[16,64,128]{2,1,0:T(8,128)(2,1)}, bf16[16,64,128]{2,1,0:T(8,128)(2,1)S(1)}, u32[]{:S(2)}, u32[]{:S(2)}) collective-permute-start(bf16[16,64,128]{2,1,0:T(8,128)(2,1)} %fusion.54), channel_id=1, source_target_pairs={{0,8},{8,16},{16,24},{24,32},{32,40},{40,48},{48,56},{56,64},{64,7... | collective-permute-start | bytes 786440 | tf_op jit(solution)/shard_map/while/body/eval_jaxpr/ppermute | solution.py:13
  362.7 11.4 %collective-permute-start = (bf16[16,64,128]{2,1,0:T(8,128)(2,1)}, bf16[16,64,128]{2,1,0:T(8,128)(2,1)S(1)}, u32[]{:S(2)}, u32[]{:S(2)}) collective-permute-start(bf16[16,64,128]{2,1,0:T(8,128)(2,1)} %fusion.54), channel_id=1, source_target_pairs={{0,8},{8,16},{16,24},{24,32},{32,40},{40,48},{48,56},{56,64},{64,7... | collective-permute-start | bytes 786440 | tf_op jit(solution)/shard_map/while/body/eval_jaxpr/ppermute | solution.py:13
  377.1 10.6 %collective-permute-start = (bf16[16,64,128]{2,1,0:T(8,128)(2,1)}, bf16[16,64,128]{2,1,0:T(8,128)(2,1)S(1)}, u32[]{:S(2)}, u32[]{:S(2)}) collective-permute-start(bf16[16,64,128]{2,1,0:T(8,128)(2,1)} %fusion.54), channel_id=1, source_target_pairs={{0,8},{8,16},{16,24},{24,32},{32,40},{40,48},{48,56},{56,64},{64,7... | collective-permute-start | bytes 786440 | tf_op jit(solution)/shard_map/while/body/eval_jaxpr/ppermute | solution.py:13
  390.5 10.6 %collective-permute-start = (bf16[16,64,128]{2,1,0:T(8,128)(2,1)}, bf16[16,64,128]{2,1,0:T(8,128)(2,1)S(1)}, u32[]{:S(2)}, u32[]{:S(2)}) collective-permute-start(bf16[16,64,128]{2,1,0:T(8,128)(2,1)} %fusion.54), channel_id=1, source_target_pairs={{0,8},{8,16},{16,24},{24,32},{32,40},{40,48},{48,56},{56,64},{64,7... | collective-permute-start | bytes 786440 | tf_op jit(solution)/shard_map/while/body/eval_jaxpr/ppermute | solution.py:13
  404.0 13.2 %collective-permute-start = (bf16[16,64,128]{2,1,0:T(8,128)(2,1)}, bf16[16,64,128]{2,1,0:T(8,128)(2,1)S(1)}, u32[]{:S(2)}, u32[]{:S(2)}) collective-permute-start(bf16[16,64,128]{2,1,0:T(8,128)(2,1)} %fusion.54), channel_id=1, source_target_pairs={{0,8},{8,16},{16,24},{24,32},{32,40},{40,48},{48,56},{56,64},{64,7... | collective-permute-start | bytes 786440 | tf_op jit(solution)/shard_map/while/body/eval_jaxpr/ppermute | solution.py:13
  420.1 12.3 %collective-permute-start = (bf16[16,64,128]{2,1,0:T(8,128)(2,1)}, bf16[16,64,128]{2,1,0:T(8,128)(2,1)S(1)}, u32[]{:S(2)}, u32[]{:S(2)}) collective-permute-start(bf16[16,64,128]{2,1,0:T(8,128)(2,1)} %fusion.54), channel_id=1, source_target_pairs={{0,8},{8,16},{16,24},{24,32},{32,40},{40,48},{48,56},{56,64},{64,7... | collective-permute-start | bytes 786440 | tf_op jit(solution)/shard_map/while/body/eval_jaxpr/ppermute | solution.py:13
  435.3 11.6 %collective-permute-start = (bf16[16,64,128]{2,1,0:T(8,128)(2,1)}, bf16[16,64,128]{2,1,0:T(8,128)(2,1)S(1)}, u32[]{:S(2)}, u32[]{:S(2)}) collective-permute-start(bf16[16,64,128]{2,1,0:T(8,128)(2,1)} %fusion.54), channel_id=1, source_target_pairs={{0,8},{8,16},{16,24},{24,32},{32,40},{40,48},{48,56},{56,64},{64,7... | collective-permute-start | bytes 786440 | tf_op jit(solution)/shard_map/while/body/eval_jaxpr/ppermute | solution.py:13
  449.9 11.5 %collective-permute-start = (bf16[16,64,128]{2,1,0:T(8,128)(2,1)}, bf16[16,64,128]{2,1,0:T(8,128)(2,1)S(1)}, u32[]{:S(2)}, u32[]{:S(2)}) collective-permute-start(bf16[16,64,128]{2,1,0:T(8,128)(2,1)} %fusion.54), channel_id=1, source_target_pairs={{0,8},{8,16},{16,24},{24,32},{32,40},{40,48},{48,56},{56,64},{64,7... | collective-permute-start | bytes 786440 | tf_op jit(solution)/shard_map/while/body/eval_jaxpr/ppermute | solution.py:13
  462.2 12.3 %copy-start.6 = (s32[64,2]{0,1:T(2,128)S(1)}, s32[64,2]{0,1:T(2,128)}, u32[]{:S(2)}) copy-start(s32[64,2]{0,1:T(2,128)} %param.22) | copy-start | bytes 1540
  470.2 12.5 %all-to-all-start = ((bf16[4,64,1024]{2,1,0:T(8,128)(2,1)}), bf16[4,64,1024]{2,1,0:T(8,128)(2,1)}, u32[]{:S(2)}, u32[]{:S(2)}) async-start(bf16[4,64,1024]{2,1,0:T(8,128)(2,1)} %copy.30), calls=%async_computation | async-start | bytes 1048576 | tf_op jit(solution)/shard_map/all_to_all | solution.py:57
  474.5 10.6 %copy-start.11 = (f32[4096]{0:T(1024)S(1)}, f32[4096]{0:T(1024)}, u32[]{:S(2)}) copy-start(f32[4096]{0:T(1024)} %param.20) | copy-start | bytes 49156
  474.5 146.8 %all-gather.2.cloned.1.call-start = ((), (), s32[]{:S(2)}) async-start(), calls=%async_computation.4 | async-start | bytes 8650752 | tf_op jit(solution)/shard_map/all_gather | solution.py:89
  482.7 1.3 copy-start.2
  484.2 0.8 copy-start.1
  495.1 373.9 %reduce-scatter.2.cloned.1.call-start = ((), (), s32[]{:S(2)}) async-start(), calls=%async_computation.5 | async-start | bytes 8650752 | tf_op jit(solution)/shard_map/reduce_scatter | solution.py:94
  621.3 8.0 copy-start.8
  621.3 8.0 copy-start.9
  640.6 0.9 copy-start.10
  869.1 11.0 %all-to-all-start.2 = ((bf16[4,8,4096]{2,1,0:T(8,128)(2,1)}), bf16[4,8,4096]{2,1,0:T(8,128)(2,1)S(1)}, u32[]{:S(2)}, u32[]{:S(2)}) async-start(bf16[4,8,4096]{2,1,0:T(8,128)(2,1)} %bitcast.84), calls=%async_computation.3 | async-start | bytes 524288 | tf_op jit(solution)/shard_map/all_to_all | solution.py:101
Sparse Core Ops, SparseCore 0:
  495.3 126.0 all-gather.1
  640.7 228.3 reduce-scatter.1
where the time goes:
time: 891 us; the launch traced here: 889 us
  waiting for transfers between devices  633 us (71%)
  other arithmetic  94.9 us (11%)
  starting transfers between devices  93.5 us (10%)
  matrix products  33.1 us (4%)
  between operations  13.6 us (2%)
  local copies, waits for them, and re-layouts  10.6 us (1%)
  blocking collectives  9.75 us (1%)
    ppermute x31, waiting for transfers between devices, shifted(): return lax.ppermute(block, axis, route)  267 us
    reduce_scatter x1, waiting for transfers between devices, body(): lax.psum_scatter(jnp.dot(fragment, down_part, preferred_element_type=jnp....  226 us
    all_gather x1, waiting for transfers between devices, body(): fragment = lax.all_gather(routed, 'seq', axis=0, tiled=True)  126 us
    ppermute x31, starting transfers between devices, shifted(): return lax.ppermute(block, axis, route)  84.9 us
    convert_element_type x31, other arithmetic, advance(): outgoing.astype(jnp.bfloat16)  63.5 us
    convert_element_type x31, other arithmetic, advance(): shifted(outgoing.astype(jnp.bfloat16), 'seq', 1).astype(outgoing.dtype)  26.7 us
  transfers between devices with their start and end apart: 35, of which 35 were waited for; matrix products, arithmetic and copies ran while one was open for 0% of the time, Pallas kernels for 0%

commit v1 on v0

--- a/solution.py
+++ b/solution.py
@@ -2,6 +2,7 @@
 import jax.numpy as jnp
 from jax import lax
 from jax.sharding import PartitionSpec as P
+from jax.lax import all_to_all, psum
 
 P_SIZE = 64
 CAP = 8
@@ -86,7 +87,9 @@
     gate_part = gate_weight[0]
     up_part = up_weight[0]
     down_part = down_weight[0]
-    fragment = lax.all_gather(routed, "seq", axis=0, tiled=True)
+    fragment = jnp.concatenate(
+        all_to_all(jnp.stack([routed for _ in range(psum(1, "seq"))], axis=0), "seq", 0, 0), 0
+    )
     gated = jnp.dot(fragment, gate_part, preferred_element_type=jnp.float32)
     lifted = jnp.dot(fragment, up_part, preferred_element_type=jnp.float32)
     hidden_all = (jax.nn.silu(gated) * lifted).astype(jnp.bfloat16)

time: 891 us -> 948 us (1.064)
  blocking collectives: 9.75 us -> 198 us
  waiting for transfers between devices: 633 us -> 505 us
    all_to_all x0 -> x1, blocking collectives: none -> 189 us  [body(): all_to_all(jnp.stack([routed for _ in range(psum(1, 'seq'))], axis=0), 's...]
    all_gather x1 -> x0, waiting for transfers between devices: 126 us -> none  [body(): fragment = lax.all_gather(routed, 'seq', axis=0, tiled=True)]
  transfers between devices with their start and end apart: 35 -> 34, of which waited for: 35 -> 34; matrix products, arithmetic and copies ran while one was open for 0% -> 0% of each run, Pallas kernels for 0% -> 0%
where the time goes in v1:
time: 948 us; the launch traced here: 946 us
  waiting for transfers between devices  505 us (53%)
  blocking collectives  198 us (21%)
  other arithmetic  94.9 us (10%)
  starting transfers between devices  93.5 us (10%)
  matrix products  29.6 us (3%)
  between operations  13.6 us (1%)
  local copies, waits for them, and re-layouts  10.9 us (1%)
    ppermute x31, waiting for transfers between devices, shifted(): return lax.ppermute(block, axis, route)  267 us
    reduce_scatter x1, waiting for transfers between devices, body(): lax.psum_scatter(jnp.dot(fragment, down_part, preferred_element_type=jnp....  224 us
    all_to_all x1, blocking collectives, body(): all_to_all(jnp.stack([routed for _ in range(psum(1, 'seq'))], axis=0), 's...  189 us
    ppermute x31, starting transfers between devices, shifted(): return lax.ppermute(block, axis, route)  84.9 us
    convert_element_type x31, other arithmetic, advance(): outgoing.astype(jnp.bfloat16)  63.5 us
    convert_element_type x31, other arithmetic, advance(): shifted(outgoing.astype(jnp.bfloat16), 'seq', 1).astype(outgoing.dtype)  26.7 us
  transfers between devices with their start and end apart: 34, of which 34 were waited for; matrix products, arithmetic and copies ran while one was open for 0% of the time, Pallas kernels for 0%

profile of v1, /device:TPU:64, one launch (start us, length us, event | category | flops | bytes accessed | tf_op | source)
XLA Modules:
  0.0 945.7 jit_solution(8559393438891140684)
XLA Ops:
  14.3 2.7 convolution_bitcast_fusion.2
  16.9 3.3 fusion.18
  20.3 442.0 %while.11 = (s32[]{:T(128)}, f32[16,64,128]{2,1,0:T(8,128)}, f32[16]{0:T(128)S(1)}, f32[16,64,128]{2,1,0:T(8,128)}, s32[]{:T(128)}, /*index=5*/s32[]{:T(128)}) while((s32[]{:T(128)}, f32[16,64,128]{2,1,0:T(8,128)}, f32[16]{0:T(128)S(1)}, f32[16,64,128]{2,1,0:T(8,128)}, s32[]{:T(128)}, /*index=5*/s32[]{:T(128)}) %tuple.31), condition=%wide.region_3.4_spmd.clone, body=%wide.region_2.3_spmd.clone.sunk | while | flops 655363 | bytes 3145911 | solution.py:51
  22.2 3.5 collective-permute-start
  25.7 8.8 collective-permute-done
  35.3 2.1 fusion.54
  39.3 9.5 %collective-permute-done = bf16[16,64,128]{2,1,0:T(8,128)(2,1)S(1)} collective-permute-done((bf16[16,64,128]{2,1,0:T(8,128)(2,1)}, bf16[16,64,128]{2,1,0:T(8,128)(2,1)S(1)}, u32[]{:S(2)}, u32[]{:S(2)}) %collective-permute-start) | collective-permute-done | bytes 262176 | tf_op jit(solution)/shard_map/while/body/eval_jaxpr/ppermute | solution.py:14
  49.6 2.1 fusion.54
  53.6 8.7 collective-permute-done
  63.1 2.1 fusion.54
  67.1 8.7 collective-permute-done
  76.6 2.1 fusion.54
  80.6 8.7 collective-permute-done
  90.1 2.1 fusion.54
  94.1 8.7 collective-permute-done
  103.6 2.1 fusion.54
  107.5 8.7 collective-permute-done
  117.1 2.1 fusion.54
  121.0 8.7 collective-permute-done
  130.5 2.1 fusion.54
  134.5 8.9 collective-permute-done
  144.2 2.1 fusion.54
  148.2 10.0 %collective-permute-done = bf16[16,64,128]{2,1,0:T(8,128)(2,1)S(1)} collective-permute-done((bf16[16,64,128]{2,1,0:T(8,128)(2,1)}, bf16[16,64,128]{2,1,0:T(8,128)(2,1)S(1)}, u32[]{:S(2)}, u32[]{:S(2)}) %collective-permute-start) | collective-permute-done | bytes 262176 | tf_op jit(solution)/shard_map/while/body/eval_jaxpr/ppermute | solution.py:14
  163.1 11.2 %collective-permute-done = bf16[16,64,128]{2,1,0:T(8,128)(2,1)S(1)} collective-permute-done((bf16[16,64,128]{2,1,0:T(8,128)(2,1)}, bf16[16,64,128]{2,1,0:T(8,128)(2,1)S(1)}, u32[]{:S(2)}, u32[]{:S(2)}) %collective-permute-start) | collective-permute-done | bytes 262176 | tf_op jit(solution)/shard_map/while/body/eval_jaxpr/ppermute | solution.py:14
  179.0 10.6 %collective-permute-done = bf16[16,64,128]{2,1,0:T(8,128)(2,1)S(1)} collective-permute-done((bf16[16,64,128]{2,1,0:T(8,128)(2,1)}, bf16[16,64,128]{2,1,0:T(8,128)(2,1)S(1)}, u32[]{:S(2)}, u32[]{:S(2)}) %collective-permute-start) | collective-permute-done | bytes 262176 | tf_op jit(solution)/shard_map/while/body/eval_jaxpr/ppermute | solution.py:14
  190.5 2.1 fusion.54
  194.5 9.8 %collective-permute-done = bf16[16,64,128]{2,1,0:T(8,128)(2,1)S(1)} collective-permute-done((bf16[16,64,128]{2,1,0:T(8,128)(2,1)}, bf16[16,64,128]{2,1,0:T(8,128)(2,1)S(1)}, u32[]{:S(2)}, u32[]{:S(2)}) %collective-permute-start) | collective-permute-done | bytes 262176 | tf_op jit(solution)/shard_map/while/body/eval_jaxpr/ppermute | solution.py:14
  209.1 8.9 collective-permute-done
  222.8 8.7 collective-permute-done
  236.3 8.7 collective-permute-done
  249.8 8.7 collective-permute-done
  263.3 8.7 collective-permute-done
  276.8 8.7 collective-permute-done
  290.3 8.7 collective-permute-done
  303.8 9.4 collective-permute-done
  318.0 10.6 %collective-permute-done = bf16[16,64,128]{2,1,0:T(8,128)(2,1)S(1)} collective-permute-done((bf16[16,64,128]{2,1,0:T(8,128)(2,1)}, bf16[16,64,128]{2,1,0:T(8,128)(2,1)S(1)}, u32[]{:S(2)}, u32[]{:S(2)}) %collective-permute-start) | collective-permute-done | bytes 262176 | tf_op jit(solution)/shard_map/while/body/eval_jaxpr/ppermute | solution.py:14
  333.4 11.2 %collective-permute-done = bf16[16,64,128]{2,1,0:T(8,128)(2,1)S(1)} collective-permute-done((bf16[16,64,128]{2,1,0:T(8,128)(2,1)}, bf16[16,64,128]{2,1,0:T(8,128)(2,1)S(1)}, u32[]{:S(2)}, u32[]{:S(2)}) %collective-permute-start) | collective-permute-done | bytes 262176 | tf_op jit(solution)/shard_map/while/body/eval_jaxpr/ppermute | solution.py:14
  349.5 10.3 %collective-permute-done = bf16[16,64,128]{2,1,0:T(8,128)(2,1)S(1)} collective-permute-done((bf16[16,64,128]{2,1,0:T(8,128)(2,1)}, bf16[16,64,128]{2,1,0:T(8,128)(2,1)S(1)}, u32[]{:S(2)}, u32[]{:S(2)}) %collective-permute-start) | collective-permute-done | bytes 262176 | tf_op jit(solution)/shard_map/while/body/eval_jaxpr/ppermute | solution.py:14
  364.7 9.5 %collective-permute-done = bf16[16,64,128]{2,1,0:T(8,128)(2,1)S(1)} collective-permute-done((bf16[16,64,128]{2,1,0:T(8,128)(2,1)}, bf16[16,64,128]{2,1,0:T(8,128)(2,1)S(1)}, u32[]{:S(2)}, u32[]{:S(2)}) %collective-permute-start) | collective-permute-done | bytes 262176 | tf_op jit(solution)/shard_map/while/body/eval_jaxpr/ppermute | solution.py:14
  379.0 8.7 collective-permute-done
  390.6 3.4 collective-permute-start
  393.9 7.2 collective-permute-done
  404.0 7.7 collective-permute-start
  411.7 5.5 collective-permute-done
  420.1 8.0 collective-permute-start
  428.1 4.3 collective-permute-done
  435.3 7.5 collective-permute-start
  442.8 4.2 collective-permute-done
  449.9 7.3 collective-permute-start
  457.2 4.2 collective-permute-done
  462.2 2.9 fusion.22
  465.2 2.8 reshape.163
  467.9 2.3 copy.30
  470.2 4.3 all-to-all-start
  474.9 7.8 all-to-all-done
  484.6 9.1 all_to_all.25
  494.7 188.9 %all_to_all.26 = bf16[32,32,4096]{2,1,0:T(8,128)(2,1)S(1)} all-to-all(bf16[32,32,4096]{2,1,0:T(8,128)(2,1)S(1)} %stack.3), channel_id=1, replica_groups=mesh['seq'=32,'exp'=4,'dp'=2] {'seq'}, dimensions={0} | all-to-all | bytes 16777216 | tf_op jit(solution)/shard_map/all_to_all | solution.py:91
  683.7 4.5 fusion.8
  688.2 4.6 multiply_convert_fusion.1
  692.8 6.7 convolution_convert_fusion
  701.7 224.0 %reduce-scatter.2.cloned.1.call-done = bf16[32,4096]{1,0:T(8,128)(2,1)} async-done(((bf16[1024,4096]{1,0:T(8,128)(2,1)}), bf16[32,4096]{1,0:T(8,128)(2,1)}) %reduce-scatter.2.cloned.1.call-update) | async-done | bytes 262160 | tf_op jit(solution)/shard_map/reduce_scatter | solution.py:97
  925.7 4.2 all-to-all-start.3
  930.0 6.7 all-to-all-done.3
  936.7 2.2 fusion.4
  (131 shorter events, 130.6 us)
Async XLA Ops:
  6.5 686.2 %copy-start = (bf16[1,384,4096]{2,1,0:T(8,128)(2,1)S(1)}, bf16[1,384,4096]{2,1,0:T(8,128)(2,1)}, u32[]{:S(2)}) copy-start(bf16[1,384,4096]{2,1,0:T(8,128)(2,1)} %param.25) | copy-start | bytes 9437188
  8.3 1.4 copy-start.4
  16.9 3.3 copy-start.5
  20.3 442.0 %copy-start.3 = (bf16[256,128]{1,0:T(8,128)(2,1)S(1)}, bf16[256,128]{1,0:T(8,128)(2,1)}, u32[]{:S(2)}) copy-start(bf16[256,128]{1,0:T(8,128)(2,1)} %param.16) | copy-start | bytes 196612
  20.3 442.0 %copy-start.7 = (f32[16]{0:T(128)S(1)}, f32[16]{0:T(128)}, u32[]{:S(2)}) copy-start(f32[16]{0:T(128)} %param.18) | copy-start | bytes 196
  22.2 12.2 %collective-permute-start = (bf16[16,64,128]{2,1,0:T(8,128)(2,1)}, bf16[16,64,128]{2,1,0:T(8,128)(2,1)S(1)}, u32[]{:S(2)}, u32[]{:S(2)}) collective-permute-start(bf16[16,64,128]{2,1,0:T(8,128)(2,1)} %fusion.54), channel_id=1, source_target_pairs={{0,8},{8,16},{16,24},{24,32},{32,40},{40,48},{48,56},{56,64},{64,7... | collective-permute-start | bytes 786440 | tf_op jit(solution)/shard_map/while/body/eval_jaxpr/ppermute | solution.py:14
  37.4 11.4 %collective-permute-start = (bf16[16,64,128]{2,1,0:T(8,128)(2,1)}, bf16[16,64,128]{2,1,0:T(8,128)(2,1)S(1)}, u32[]{:S(2)}, u32[]{:S(2)}) collective-permute-start(bf16[16,64,128]{2,1,0:T(8,128)(2,1)} %fusion.54), channel_id=1, source_target_pairs={{0,8},{8,16},{16,24},{24,32},{32,40},{40,48},{48,56},{56,64},{64,7... | collective-permute-start | bytes 786440 | tf_op jit(solution)/shard_map/while/body/eval_jaxpr/ppermute | solution.py:14
  51.7 10.6 %collective-permute-start = (bf16[16,64,128]{2,1,0:T(8,128)(2,1)}, bf16[16,64,128]{2,1,0:T(8,128)(2,1)S(1)}, u32[]{:S(2)}, u32[]{:S(2)}) collective-permute-start(bf16[16,64,128]{2,1,0:T(8,128)(2,1)} %fusion.54), channel_id=1, source_target_pairs={{0,8},{8,16},{16,24},{24,32},{32,40},{40,48},{48,56},{56,64},{64,7... | collective-permute-start | bytes 786440 | tf_op jit(solution)/shard_map/while/body/eval_jaxpr/ppermute | solution.py:14
  65.2 10.6 %collective-permute-start = (bf16[16,64,128]{2,1,0:T(8,128)(2,1)}, bf16[16,64,128]{2,1,0:T(8,128)(2,1)S(1)}, u32[]{:S(2)}, u32[]{:S(2)}) collective-permute-start(bf16[16,64,128]{2,1,0:T(8,128)(2,1)} %fusion.54), channel_id=1, source_target_pairs={{0,8},{8,16},{16,24},{24,32},{32,40},{40,48},{48,56},{56,64},{64,7... | collective-permute-start | bytes 786440 | tf_op jit(solution)/shard_map/while/body/eval_jaxpr/ppermute | solution.py:14
  78.6 10.6 %collective-permute-start = (bf16[16,64,128]{2,1,0:T(8,128)(2,1)}, bf16[16,64,128]{2,1,0:T(8,128)(2,1)S(1)}, u32[]{:S(2)}, u32[]{:S(2)}) collective-permute-start(bf16[16,64,128]{2,1,0:T(8,128)(2,1)} %fusion.54), channel_id=1, source_target_pairs={{0,8},{8,16},{16,24},{24,32},{32,40},{40,48},{48,56},{56,64},{64,7... | collective-permute-start | bytes 786440 | tf_op jit(solution)/shard_map/while/body/eval_jaxpr/ppermute | solution.py:14
  92.1 10.6 %collective-permute-start = (bf16[16,64,128]{2,1,0:T(8,128)(2,1)}, bf16[16,64,128]{2,1,0:T(8,128)(2,1)S(1)}, u32[]{:S(2)}, u32[]{:S(2)}) collective-permute-start(bf16[16,64,128]{2,1,0:T(8,128)(2,1)} %fusion.54), channel_id=1, source_target_pairs={{0,8},{8,16},{16,24},{24,32},{32,40},{40,48},{48,56},{56,64},{64,7... | collective-permute-start | bytes 786440 | tf_op jit(solution)/shard_map/while/body/eval_jaxpr/ppermute | solution.py:14
  105.6 10.6 %collective-permute-start = (bf16[16,64,128]{2,1,0:T(8,128)(2,1)}, bf16[16,64,128]{2,1,0:T(8,128)(2,1)S(1)}, u32[]{:S(2)}, u32[]{:S(2)}) collective-permute-start(bf16[16,64,128]{2,1,0:T(8,128)(2,1)} %fusion.54), channel_id=1, source_target_pairs={{0,8},{8,16},{16,24},{24,32},{32,40},{40,48},{48,56},{56,64},{64,7... | collective-permute-start | bytes 786440 | tf_op jit(solution)/shard_map/while/body/eval_jaxpr/ppermute | solution.py:14
  119.1 10.6 %collective-permute-start = (bf16[16,64,128]{2,1,0:T(8,128)(2,1)}, bf16[16,64,128]{2,1,0:T(8,128)(2,1)S(1)}, u32[]{:S(2)}, u32[]{:S(2)}) collective-permute-start(bf16[16,64,128]{2,1,0:T(8,128)(2,1)} %fusion.54), channel_id=1, source_target_pairs={{0,8},{8,16},{16,24},{24,32},{32,40},{40,48},{48,56},{56,64},{64,7... | collective-permute-start | bytes 786440 | tf_op jit(solution)/shard_map/while/body/eval_jaxpr/ppermute | solution.py:14
  132.6 10.8 %collective-permute-start = (bf16[16,64,128]{2,1,0:T(8,128)(2,1)}, bf16[16,64,128]{2,1,0:T(8,128)(2,1)S(1)}, u32[]{:S(2)}, u32[]{:S(2)}) collective-permute-start(bf16[16,64,128]{2,1,0:T(8,128)(2,1)} %fusion.54), channel_id=1, source_target_pairs={{0,8},{8,16},{16,24},{24,32},{32,40},{40,48},{48,56},{56,64},{64,7... | collective-permute-start | bytes 786440 | tf_op jit(solution)/shard_map/while/body/eval_jaxpr/ppermute | solution.py:14
  146.3 11.9 %collective-permute-start = (bf16[16,64,128]{2,1,0:T(8,128)(2,1)}, bf16[16,64,128]{2,1,0:T(8,128)(2,1)S(1)}, u32[]{:S(2)}, u32[]{:S(2)}) collective-permute-start(bf16[16,64,128]{2,1,0:T(8,128)(2,1)} %fusion.54), channel_id=1, source_target_pairs={{0,8},{8,16},{16,24},{24,32},{32,40},{40,48},{48,56},{56,64},{64,7... | collective-permute-start | bytes 786440 | tf_op jit(solution)/shard_map/while/body/eval_jaxpr/ppermute | solution.py:14
  161.1 13.1 %collective-permute-start = (bf16[16,64,128]{2,1,0:T(8,128)(2,1)}, bf16[16,64,128]{2,1,0:T(8,128)(2,1)S(1)}, u32[]{:S(2)}, u32[]{:S(2)}) collective-permute-start(bf16[16,64,128]{2,1,0:T(8,128)(2,1)} %fusion.54), channel_id=1, source_target_pairs={{0,8},{8,16},{16,24},{24,32},{32,40},{40,48},{48,56},{56,64},{64,7... | collective-permute-start | bytes 786440 | tf_op jit(solution)/shard_map/while/body/eval_jaxpr/ppermute | solution.py:14
  177.1 12.5 %collective-permute-start = (bf16[16,64,128]{2,1,0:T(8,128)(2,1)}, bf16[16,64,128]{2,1,0:T(8,128)(2,1)S(1)}, u32[]{:S(2)}, u32[]{:S(2)}) collective-permute-start(bf16[16,64,128]{2,1,0:T(8,128)(2,1)} %fusion.54), channel_id=1, source_target_pairs={{0,8},{8,16},{16,24},{24,32},{32,40},{40,48},{48,56},{56,64},{64,7... | collective-permute-start | bytes 786440 | tf_op jit(solution)/shard_map/while/body/eval_jaxpr/ppermute | solution.py:14
  192.6 11.7 %collective-permute-start = (bf16[16,64,128]{2,1,0:T(8,128)(2,1)}, bf16[16,64,128]{2,1,0:T(8,128)(2,1)S(1)}, u32[]{:S(2)}, u32[]{:S(2)}) collective-permute-start(bf16[16,64,128]{2,1,0:T(8,128)(2,1)} %fusion.54), channel_id=1, source_target_pairs={{0,8},{8,16},{16,24},{24,32},{32,40},{40,48},{48,56},{56,64},{64,7... | collective-permute-start | bytes 786440 | tf_op jit(solution)/shard_map/while/body/eval_jaxpr/ppermute | solution.py:14
  207.2 10.8 %collective-permute-start = (bf16[16,64,128]{2,1,0:T(8,128)(2,1)}, bf16[16,64,128]{2,1,0:T(8,128)(2,1)S(1)}, u32[]{:S(2)}, u32[]{:S(2)}) collective-permute-start(bf16[16,64,128]{2,1,0:T(8,128)(2,1)} %fusion.54), channel_id=1, source_target_pairs={{0,8},{8,16},{16,24},{24,32},{32,40},{40,48},{48,56},{56,64},{64,7... | collective-permute-start | bytes 786440 | tf_op jit(solution)/shard_map/while/body/eval_jaxpr/ppermute | solution.py:14
  220.9 10.6 %collective-permute-start = (bf16[16,64,128]{2,1,0:T(8,128)(2,1)}, bf16[16,64,128]{2,1,0:T(8,128)(2,1)S(1)}, u32[]{:S(2)}, u32[]{:S(2)}) collective-permute-start(bf16[16,64,128]{2,1,0:T(8,128)(2,1)} %fusion.54), channel_id=1, source_target_pairs={{0,8},{8,16},{16,24},{24,32},{32,40},{40,48},{48,56},{56,64},{64,7... | collective-permute-start | bytes 786440 | tf_op jit(solution)/shard_map/while/body/eval_jaxpr/ppermute | solution.py:14
  234.4 10.6 %collective-permute-start = (bf16[16,64,128]{2,1,0:T(8,128)(2,1)}, bf16[16,64,128]{2,1,0:T(8,128)(2,1)S(1)}, u32[]{:S(2)}, u32[]{:S(2)}) collective-permute-start(bf16[16,64,128]{2,1,0:T(8,128)(2,1)} %fusion.54), channel_id=1, source_target_pairs={{0,8},{8,16},{16,24},{24,32},{32,40},{40,48},{48,56},{56,64},{64,7... | collective-permute-start | bytes 786440 | tf_op jit(solution)/shard_map/while/body/eval_jaxpr/ppermute | solution.py:14
  247.9 10.6 %collective-permute-start = (bf16[16,64,128]{2,1,0:T(8,128)(2,1)}, bf16[16,64,128]{2,1,0:T(8,128)(2,1)S(1)}, u32[]{:S(2)}, u32[]{:S(2)}) collective-permute-start(bf16[16,64,128]{2,1,0:T(8,128)(2,1)} %fusion.54), channel_id=1, source_target_pairs={{0,8},{8,16},{16,24},{24,32},{32,40},{40,48},{48,56},{56,64},{64,7... | collective-permute-start | bytes 786440 | tf_op jit(solution)/shard_map/while/body/eval_jaxpr/ppermute | solution.py:14
  261.4 10.6 %collective-permute-start = (bf16[16,64,128]{2,1,0:T(8,128)(2,1)}, bf16[16,64,128]{2,1,0:T(8,128)(2,1)S(1)}, u32[]{:S(2)}, u32[]{:S(2)}) collective-permute-start(bf16[16,64,128]{2,1,0:T(8,128)(2,1)} %fusion.54), channel_id=1, source_target_pairs={{0,8},{8,16},{16,24},{24,32},{32,40},{40,48},{48,56},{56,64},{64,7... | collective-permute-start | bytes 786440 | tf_op jit(solution)/shard_map/while/body/eval_jaxpr/ppermute | solution.py:14
  274.9 10.6 %collective-permute-start = (bf16[16,64,128]{2,1,0:T(8,128)(2,1)}, bf16[16,64,128]{2,1,0:T(8,128)(2,1)S(1)}, u32[]{:S(2)}, u32[]{:S(2)}) collective-permute-start(bf16[16,64,128]{2,1,0:T(8,128)(2,1)} %fusion.54), channel_id=1, source_target_pairs={{0,8},{8,16},{16,24},{24,32},{32,40},{40,48},{48,56},{56,64},{64,7... | collective-permute-start | bytes 786440 | tf_op jit(solution)/shard_map/while/body/eval_jaxpr/ppermute | solution.py:14
  288.4 10.6 %collective-permute-start = (bf16[16,64,128]{2,1,0:T(8,128)(2,1)}, bf16[16,64,128]{2,1,0:T(8,128)(2,1)S(1)}, u32[]{:S(2)}, u32[]{:S(2)}) collective-permute-start(bf16[16,64,128]{2,1,0:T(8,128)(2,1)} %fusion.54), channel_id=1, source_target_pairs={{0,8},{8,16},{16,24},{24,32},{32,40},{40,48},{48,56},{56,64},{64,7... | collective-permute-start | bytes 786440 | tf_op jit(solution)/shard_map/while/body/eval_jaxpr/ppermute | solution.py:14
  301.9 11.3 %collective-permute-start = (bf16[16,64,128]{2,1,0:T(8,128)(2,1)}, bf16[16,64,128]{2,1,0:T(8,128)(2,1)S(1)}, u32[]{:S(2)}, u32[]{:S(2)}) collective-permute-start(bf16[16,64,128]{2,1,0:T(8,128)(2,1)} %fusion.54), channel_id=1, source_target_pairs={{0,8},{8,16},{16,24},{24,32},{32,40},{40,48},{48,56},{56,64},{64,7... | collective-permute-start | bytes 786440 | tf_op jit(solution)/shard_map/while/body/eval_jaxpr/ppermute | solution.py:14
  316.1 12.5 %collective-permute-start = (bf16[16,64,128]{2,1,0:T(8,128)(2,1)}, bf16[16,64,128]{2,1,0:T(8,128)(2,1)S(1)}, u32[]{:S(2)}, u32[]{:S(2)}) collective-permute-start(bf16[16,64,128]{2,1,0:T(8,128)(2,1)} %fusion.54), channel_id=1, source_target_pairs={{0,8},{8,16},{16,24},{24,32},{32,40},{40,48},{48,56},{56,64},{64,7... | collective-permute-start | bytes 786440 | tf_op jit(solution)/shard_map/while/body/eval_jaxpr/ppermute | solution.py:14
  331.5 13.1 %collective-permute-start = (bf16[16,64,128]{2,1,0:T(8,128)(2,1)}, bf16[16,64,128]{2,1,0:T(8,128)(2,1)S(1)}, u32[]{:S(2)}, u32[]{:S(2)}) collective-permute-start(bf16[16,64,128]{2,1,0:T(8,128)(2,1)} %fusion.54), channel_id=1, source_target_pairs={{0,8},{8,16},{16,24},{24,32},{32,40},{40,48},{48,56},{56,64},{64,7... | collective-permute-start | bytes 786440 | tf_op jit(solution)/shard_map/while/body/eval_jaxpr/ppermute | solution.py:14
  347.6 12.3 %collective-permute-start = (bf16[16,64,128]{2,1,0:T(8,128)(2,1)}, bf16[16,64,128]{2,1,0:T(8,128)(2,1)S(1)}, u32[]{:S(2)}, u32[]{:S(2)}) collective-permute-start(bf16[16,64,128]{2,1,0:T(8,128)(2,1)} %fusion.54), channel_id=1, source_target_pairs={{0,8},{8,16},{16,24},{24,32},{32,40},{40,48},{48,56},{56,64},{64,7... | collective-permute-start | bytes 786440 | tf_op jit(solution)/shard_map/while/body/eval_jaxpr/ppermute | solution.py:14
  362.7 11.4 %collective-permute-start = (bf16[16,64,128]{2,1,0:T(8,128)(2,1)}, bf16[16,64,128]{2,1,0:T(8,128)(2,1)S(1)}, u32[]{:S(2)}, u32[]{:S(2)}) collective-permute-start(bf16[16,64,128]{2,1,0:T(8,128)(2,1)} %fusion.54), channel_id=1, source_target_pairs={{0,8},{8,16},{16,24},{24,32},{32,40},{40,48},{48,56},{56,64},{64,7... | collective-permute-start | bytes 786440 | tf_op jit(solution)/shard_map/while/body/eval_jaxpr/ppermute | solution.py:14
  377.1 10.6 %collective-permute-start = (bf16[16,64,128]{2,1,0:T(8,128)(2,1)}, bf16[16,64,128]{2,1,0:T(8,128)(2,1)S(1)}, u32[]{:S(2)}, u32[]{:S(2)}) collective-permute-start(bf16[16,64,128]{2,1,0:T(8,128)(2,1)} %fusion.54), channel_id=1, source_target_pairs={{0,8},{8,16},{16,24},{24,32},{32,40},{40,48},{48,56},{56,64},{64,7... | collective-permute-start | bytes 786440 | tf_op jit(solution)/shard_map/while/body/eval_jaxpr/ppermute | solution.py:14
  390.6 10.6 %collective-permute-start = (bf16[16,64,128]{2,1,0:T(8,128)(2,1)}, bf16[16,64,128]{2,1,0:T(8,128)(2,1)S(1)}, u32[]{:S(2)}, u32[]{:S(2)}) collective-permute-start(bf16[16,64,128]{2,1,0:T(8,128)(2,1)} %fusion.54), channel_id=1, source_target_pairs={{0,8},{8,16},{16,24},{24,32},{32,40},{40,48},{48,56},{56,64},{64,7... | collective-permute-start | bytes 786440 | tf_op jit(solution)/shard_map/while/body/eval_jaxpr/ppermute | solution.py:14
  404.0 13.2 %collective-permute-start = (bf16[16,64,128]{2,1,0:T(8,128)(2,1)}, bf16[16,64,128]{2,1,0:T(8,128)(2,1)S(1)}, u32[]{:S(2)}, u32[]{:S(2)}) collective-permute-start(bf16[16,64,128]{2,1,0:T(8,128)(2,1)} %fusion.54), channel_id=1, source_target_pairs={{0,8},{8,16},{16,24},{24,32},{32,40},{40,48},{48,56},{56,64},{64,7... | collective-permute-start | bytes 786440 | tf_op jit(solution)/shard_map/while/body/eval_jaxpr/ppermute | solution.py:14
  420.1 12.3 %collective-permute-start = (bf16[16,64,128]{2,1,0:T(8,128)(2,1)}, bf16[16,64,128]{2,1,0:T(8,128)(2,1)S(1)}, u32[]{:S(2)}, u32[]{:S(2)}) collective-permute-start(bf16[16,64,128]{2,1,0:T(8,128)(2,1)} %fusion.54), channel_id=1, source_target_pairs={{0,8},{8,16},{16,24},{24,32},{32,40},{40,48},{48,56},{56,64},{64,7... | collective-permute-start | bytes 786440 | tf_op jit(solution)/shard_map/while/body/eval_jaxpr/ppermute | solution.py:14
  435.3 11.6 %collective-permute-start = (bf16[16,64,128]{2,1,0:T(8,128)(2,1)}, bf16[16,64,128]{2,1,0:T(8,128)(2,1)S(1)}, u32[]{:S(2)}, u32[]{:S(2)}) collective-permute-start(bf16[16,64,128]{2,1,0:T(8,128)(2,1)} %fusion.54), channel_id=1, source_target_pairs={{0,8},{8,16},{16,24},{24,32},{32,40},{40,48},{48,56},{56,64},{64,7... | collective-permute-start | bytes 786440 | tf_op jit(solution)/shard_map/while/body/eval_jaxpr/ppermute | solution.py:14
  449.9 11.5 %collective-permute-start = (bf16[16,64,128]{2,1,0:T(8,128)(2,1)}, bf16[16,64,128]{2,1,0:T(8,128)(2,1)S(1)}, u32[]{:S(2)}, u32[]{:S(2)}) collective-permute-start(bf16[16,64,128]{2,1,0:T(8,128)(2,1)} %fusion.54), channel_id=1, source_target_pairs={{0,8},{8,16},{16,24},{24,32},{32,40},{40,48},{48,56},{56,64},{64,7... | collective-permute-start | bytes 786440 | tf_op jit(solution)/shard_map/while/body/eval_jaxpr/ppermute | solution.py:14
  462.2 12.3 %copy-start.6 = (s32[64,2]{0,1:T(2,128)S(1)}, s32[64,2]{0,1:T(2,128)}, u32[]{:S(2)}) copy-start(s32[64,2]{0,1:T(2,128)} %param.22) | copy-start | bytes 1540
  470.2 12.5 %all-to-all-start = ((bf16[4,64,1024]{2,1,0:T(8,128)(2,1)}), bf16[4,64,1024]{2,1,0:T(8,128)(2,1)}, u32[]{:S(2)}, u32[]{:S(2)}) async-start(bf16[4,64,1024]{2,1,0:T(8,128)(2,1)} %copy.30), calls=%async_computation | async-start | bytes 1048576 | tf_op jit(solution)/shard_map/all_to_all | solution.py:58
  474.5 9.8 %copy-start.11 = (f32[4096]{0:T(1024)S(1)}, f32[4096]{0:T(1024)}, u32[]{:S(2)}) copy-start(f32[4096]{0:T(1024)} %param.20) | copy-start | bytes 49156
  474.5 451.2 %reduce-scatter.2.cloned.1.call-start = ((), (), s32[]{:S(2)}) async-start(), calls=%async_computation.5 | async-start | bytes 8650752 | tf_op jit(solution)/shard_map/reduce_scatter | solution.py:97
  482.7 1.3 copy-start.2
  484.3 9.4 copy-start.1
  494.7 188.9 %copy-start.8 = (bf16[1,4096,384]{2,1,0:T(8,128)(2,1)S(1)}, bf16[1,4096,384]{2,1,0:T(8,128)(2,1)}, u32[]{:S(2)}) copy-start(bf16[1,4096,384]{2,1,0:T(8,128)(2,1)} %param.23) | copy-start | bytes 9437188
  683.7 4.5 copy-start.9
  699.4 0.9 copy-start.10
  925.7 10.9 %all-to-all-start.3 = ((bf16[4,8,4096]{2,1,0:T(8,128)(2,1)}), bf16[4,8,4096]{2,1,0:T(8,128)(2,1)S(1)}, u32[]{:S(2)}, u32[]{:S(2)}) async-start(bf16[4,8,4096]{2,1,0:T(8,128)(2,1)} %bitcast.87), calls=%async_computation.4 | async-start | bytes 524288 | tf_op jit(solution)/shard_map/all_to_all | solution.py:104
Sparse Core Ops, SparseCore 0:
  699.6 226.1 reduce-scatter.1
